TPU v7x, 256 devices: a whole 4x4x8 slice. The times are simulated.
256 devices in a mesh: tok: 8 (over y, x_hi), hid: 32 (over x_lo, z, core).
Axes of the slice: x: 4 (x_hi: 2, x_lo: 2; x = x_hi * 2 + x_lo), y: 4, z: 8, core: 2. Of those that a mesh axis runs over, the one named last changes fastest.
Arguments:
- activations: bfloat16 [8192, 4096], P('tok', 'hid'), may hold values from -6 to 6
- gate_weight: bfloat16 [4096, 14336], P(None, 'hid'), may hold values from -0.09375 to 0.09375
- up_weight: bfloat16 [4096, 14336], P(None, 'hid'), may hold values from -0.09375 to 0.09375
- row_signs: int32 [8192], P('tok'), may hold values from 0 to 1
- row_scales: float32 [8192], P('tok'), may hold values from 0.25 to 4
- kept_rows: int32 [512], P('tok'), may hold values from 0 to 1023, as said below
Outputs:
- gram_matrix: float32 [512, 512], P('tok')
Inputs may be any that keep to these rules, and one draw needn't show every extreme that they name: `kept_rows`: within each aligned block of 64 entries the values are distinct.
All inputs are finite; a program needn't handle non-finite values.
Results may differ from a plain program's by a relative error of at most 0.0014.
Values may be sent and summed in bfloat16 or wider, within the bound.
A program may use at most 64 MiB of HBM per device.

v0:
```python
import jax
import jax.numpy as jnp
from jax import lax
from jax.sharding import PartitionSpec as P

FF = 14336


def in_order(tiles, dim):
    tiles = jnp.moveaxis(tiles, 0, dim)
    dims = tiles.shape
    return tiles.reshape(*dims[:dim], dims[dim] * dims[dim + 1], *dims[dim + 2 :])


def from_everyone(array, axis):
    copies = jnp.broadcast_to(array, (lax.axis_size(axis), *array.shape))
    return lax.all_to_all(copies, axis, split_axis=0, concat_axis=0, tiled=True)


def gather_directly(array, axis, dim):
    return in_order(from_everyone(array, axis), dim)


def split_up(array, dim, peers):
    before, after = (array.shape[:dim], array.shape[dim + 1 :])
    return jnp.moveaxis(array.reshape(*before, peers, -1, *after), dim, 0)


def summed_on_arrival(array, axis, dim):
    peers = lax.axis_size(axis)
    tiles = lax.all_to_all(split_up(array, dim, peers), axis, 0, 0, tiled=True)
    return jnp.sum(tiles, axis=0)


def filled_up(lines, peers):
    spare = -len(lines) % peers
    return jnp.pad(lines, [(0, spare)] + [(0, 0)] * (lines.ndim - 1))


def nested_sum(array, axes):
    lines = array.reshape(-1, array.shape[-1])
    padded = filled_up(lines, lax.axis_size(axes))
    whole = gather_directly(summed_on_arrival(padded, axes, 0), axes, 0)
    return lax.slice_in_dim(whole, 0, len(lines)).reshape(array.shape)


def bit_parity(values):
    parity = jnp.zeros_like(values)
    for shift_count in range(16):
        parity = parity ^ values >> shift_count & 1
    return parity


def hadamard_signs(first_rows, columns):
    parity = bit_parity(first_rows[:, None] & columns[None, :])
    return 1 - 2 * parity


def per_device(activations, gate_weight, up_weight, row_signs, row_scales, kept_rows):
    tok_rows = activations.shape[0]
    kept_count = kept_rows.shape[0]
    shard_count = lax.axis_size("tok")
    position = lax.axis_index("tok")
    row_scale = float(tok_rows * shard_count) ** (-0.5)
    shard_cols = lax.all_gather(activations, "hid", axis=1, tiled=True)
    gate_proj = jnp.dot(shard_cols, gate_weight, preferred_element_type=jnp.float32)
    up_proj = jnp.dot(shard_cols, up_weight, preferred_element_type=jnp.float32)
    row_factor = (2 * row_signs - 1).astype(jnp.float32) * row_scales
    signed_hidden = (row_factor[:, None] * jax.nn.silu(gate_proj) * up_proj).astype(jnp.bfloat16)
    local_positions = jnp.arange(tok_rows, dtype=jnp.int32)
    every_kept = gather_directly(kept_rows, "tok", 0)
    owners = jnp.arange(kept_count * lax.axis_size("tok"), dtype=jnp.int32) // kept_count
    signs_table = hadamard_signs(every_kept, local_positions).astype(jnp.bfloat16)
    partial_rows = jnp.dot(signs_table, signed_hidden, preferred_element_type=jnp.float32)
    owner_parity = bit_parity(owners & position)
    owner_sign = (1 - 2 * owner_parity).astype(jnp.float32)
    kept_values = summed_on_arrival(partial_rows * owner_sign[:, None], "tok", 0)
    sketch = (kept_values * row_scale).astype(jnp.bfloat16)
    gram_part = lax.dot_general(
        sketch,
        gather_directly(sketch, "tok", 0),
        (((1,), (1,)), ((), ())),
        preferred_element_type=jnp.float32,
    )
    gram_matrix = nested_sum(gram_part * float(FF) ** (-0.5), "hid")
    return gram_matrix


def solution(mesh):
    placed = (P("tok", "hid"), P(None, "hid"), P(None, "hid"), P("tok"), P("tok"), P("tok"))
    return jax.shard_map(
        per_device, mesh=mesh, in_specs=placed, out_specs=P("tok", None), check_vma=False
    )
```

profile of v0, /device:TPU:1, one launch (start us, length us, event | category | flops | bytes accessed | tf_op | source)
XLA Modules:
  0.0 198.6 jit_solution(16308631129207725053)
XLA Ops:
  6.5 0.0 all-gather.2.cloned.1.call-start
  6.5 0.7 all-gather.2.cloned.1.call-update
  7.3 1.3 broadcast_in_dim.12
  8.5 7.5 %all-to-all-start = ((s32[8,1,64]{2,1,0:T(1,128)}), s32[8,1,64]{2,1,0:T(1,128)S(1)}, u32[]{:S(2)}, u32[]{:S(2)}) async-start(s32[8,1,64]{2,1,0:T(1,128)} %broadcast_in_dim.12), calls=%async_computation | async-start | bytes 8192 | tf_op jit(solution)/shard_map/all_to_all | solution.py:17
  16.0 0.7 convert_multiply_fusion
  16.7 5.7 %all-to-all-done = s32[8,1,64]{2,1,0:T(1,128)S(1)} async-done(((s32[8,1,64]{2,1,0:T(1,128)}), s32[8,1,64]{2,1,0:T(1,128)S(1)}, u32[]{:S(2)}, u32[]{:S(2)}) %all-to-all-start) | async-done | bytes 2080 | tf_op jit(solution)/shard_map/all_to_all | solution.py:17
  22.4 0.5 broadcast.213
  22.9 0.7 reduce.3
  23.6 0.1 and.199
  23.7 79.6 %all-gather.2.cloned.1.call-done = bf16[1024,4096]{1,0:T(8,128)(2,1)} async-done(((bf16[1024,128]{1,0:T(8,128)(2,1)}), bf16[1024,4096]{1,0:T(8,128)(2,1)}) %all-gather.2.cloned.1.call-update) | async-done | bytes 8388624 | tf_op jit(solution)/shard_map/all_gather | solution.py:65
  103.2 9.7 %fusion.40 = f32[1024,448]{0,1:T(8,128)} fusion(bf16[1024,4096]{1,0:T(8,128)(2,1)} %all-gather.2.cloned.1.call-done, bf16[4096,448]{0,1:T(8,128)(2,1)} %param.7), kind=kOutput, calls=%fused_computation.51 | convolution fusion | flops 3758096384 | bytes 13893632 | tf_op jit(solution)/shard_map/dot_general | solution.py:66
  113.0 12.8 %convolution_multiply_fusion = f32[512,448]{0,1:T(8,128)S(1)} fusion(f32[1024,448]{0,1:T(8,128)} %fusion.40, bf16[1024,4096]{1,0:T(8,128)(2,1)} %all-gather.2.cloned.1.call-done, bf16[4096,448]{0,1:T(8,128)(2,1)} %param.8, s32[512]{0:T(512)S(1)} %and.199, f32[1024]{0:T(1024)S(1)} %convert_multiply_fusion, f32[512]{0:T(512)S(1)} %subtract_convert_fusion.2), kind=kOutput, calls=%fused_computation.2 | convolution fusion | flops 4258037760 | bytes 14819328 | tf_op jit(solution)/shard_map/dot_general | solution.py:74
  125.7 0.3 copy.7
  126.1 21.6 %all_to_all.26 = f32[8,64,448]{2,1,0:T(8,128)S(1)} all-to-all(f32[8,64,448]{2,1,0:T(8,128)S(1)} %bitcast.8), channel_id=1, replica_groups=mesh['tok'=8,'hid'=32] {'tok'}, dimensions={0} | all-to-all | bytes 1835008 | tf_op jit(solution)/shard_map/all_to_all | solution.py:31
  147.7 0.1 reduce_sum.18
  147.9 13.0 %all_to_all.27 = bf16[8,64,448]{2,1,0:T(8,128)(2,1)S(1)} all-to-all(bf16[8,64,448]{2,1,0:T(8,128)(2,1)S(1)} %broadcast_in_dim.13), channel_id=1, replica_groups=mesh['tok'=8,'hid'=32] {'tok'}, dimensions={0} | all-to-all | bytes 917504 | tf_op jit(solution)/shard_map/all_to_all | solution.py:17
  160.8 0.3 convolution_multiply_fusion.1
  161.1 0.1 reshape.85
  161.2 16.3 %all_to_all.28 = f32[32,2,512]{2,1,0:T(2,128)S(1)} all-to-all(f32[32,2,512]{2,1,0:T(2,128)S(1)} %reshape.85), channel_id=1, replica_groups=mesh['tok'=8,'hid'=32] {'hid'}, dimensions={0} | all-to-all | bytes 262144 | tf_op jit(solution)/shard_map/all_to_all | solution.py:31
  177.5 0.1 reduce_sum.19
  177.6 13.4 %all_to_all.29 = f32[32,2,512]{2,1,0:T(2,128)S(1)} all-to-all(f32[32,2,512]{2,1,0:T(2,128)S(1)} %broadcast_in_dim.14), channel_id=1, replica_groups=mesh['tok'=8,'hid'=32] {'hid'}, dimensions={0} | all-to-all | bytes 262144 | tf_op jit(solution)/shard_map/all_to_all | solution.py:17
  191.0 0.7 reshape.86
  (4 shorter events, 0.1 us)
Async XLA Ops:
  6.5 96.7 %all-gather.2.cloned.1.call-start = ((), (), s32[]{:S(2)}) async-start(), calls=%async_computation.5 | async-start | bytes 8650752 | tf_op jit(solution)/shard_map/all_gather | solution.py:65
  8.5 13.9 %all-to-all-start = ((s32[8,1,64]{2,1,0:T(1,128)}), s32[8,1,64]{2,1,0:T(1,128)S(1)}, u32[]{:S(2)}, u32[]{:S(2)}) async-start(s32[8,1,64]{2,1,0:T(1,128)} %broadcast_in_dim.12), calls=%async_computation | async-start | bytes 8192 | tf_op jit(solution)/shard_map/all_to_all | solution.py:17
Sparse Core Ops, SparseCore 0:
  9.1 94.0 all-gather.1
where the time goes:
time: 199 us
  waiting for transfers between devices  86 us (43%)
  blocking collectives  64.3 us (32%)
  matrix products  22.8 us (11%)
  between operations  13.5 us (7%)
  starting transfers between devices  7.48 us (4%)
  local copies, waits for them, and re-layouts  3.06 us (2%)
    all_gather x1, waiting for transfers between devices, per_device(): shard_cols = lax.all_gather(activations, 'hid', axis=1, tiled=True)  79.6 us
    all_to_all x2, blocking collectives, summed_on_arrival(): tiles = lax.all_to_all(split_up(array, dim, peers), axis, 0, 0, tiled=True)  38 us
    all_to_all x2, blocking collectives, from_everyone(): return lax.all_to_all(copies, axis, split_axis=0, concat_axis=0, tiled=True)  26.4 us
    dot_general x1, matrix products, per_device(): jnp.dot(signs_table, signed_hidden, preferred_element_type=jnp.float32)  12.8 us
    dot_general x1, matrix products, per_device(): jnp.dot(shard_cols, gate_weight, preferred_element_type=jnp.float32)  9.71 us
    all_to_all x1, starting transfers between devices, from_everyone(): return lax.all_to_all(copies, axis, split_axis=0, concat_axis=0, tiled=True)  7.48 us
    all_to_all x1, waiting for transfers between devices, from_everyone(): return lax.all_to_all(copies, axis, split_axis=0, concat_axis=0, tiled=True)  5.7 us
  transfers between devices with their start and end apart: 2, of which 2 were waited for; matrix products, arithmetic and copies ran while one was open for 2% of the time, Pallas kernels for 0%

commit v1 on v0

v1 whole, which is shorter than its diff:
```python
import functools

import jax
import jax.numpy as jnp
from jax import lax
from jax.experimental import pallas as pl
from jax.experimental.pallas import tpu as pltpu
from jax.sharding import PartitionSpec as P

FF = 14336
MESH = pl.DeviceIdType.MESH
F32 = jnp.float32
BF16 = jnp.bfloat16
ROWS_STEP = 256


def bit_parity(value):
    for shift in (8, 4, 2, 1):
        value = value ^ (value >> shift)
    return value & 1


def diagonal_column(row, count):
    ids = lax.broadcasted_iota(jnp.int32, (count, count), 0)
    lanes = lax.broadcasted_iota(jnp.int32, (count, count), 1)
    spread = jnp.where(ids == lanes, jnp.broadcast_to(row, (count, count)), 0.0)
    return jnp.sum(spread, axis=1, keepdims=True)


def fused(
    tok_n, hid_n, row_scale, gram_scale,
    act_in, wg_in, wu_in, sgn_in, scl_in, kept_in, out_ref,
    act, wg, wu, accg, accu, fcol, table, hidden, sgn, scl, kept,
    part, got, sk, gs, gr, gf,
    load_sem, zs, zr, xs, xr, ss, sr, bulk_s, bulk_r,
):
    zn = hid_n // 4
    far = zn // 2
    tokens, width = act_in.shape
    half = tokens // 2
    rows_step = min(ROWS_STEP, half)
    depth = 2 * width
    kept_n = kept.shape[-1]
    tok = lax.axis_index("tok")
    hid = lax.axis_index("hid")
    core = lax.rem(hid, 2)
    here = lax.div(hid, 2)
    z = lax.rem(here, zn)
    col = lax.div(here, zn)
    way = 1 - 2 * core

    def chip(own, d):
        c = col if own else 1 - col
        return c * zn + lax.rem(z - d * way + 2 * zn, zn)

    def at_hid(q):
        return {"hid": q * 2 + core}

    ahead = at_hid(chip(True, -1))
    behind = at_hid(chip(True, 1))
    across = at_hid(chip(False, 0))
    sibling = {"hid": here * 2 + 1 - core}

    loads = [
        pltpu.make_async_copy(act_in.at[pl.ds(h * half, half), :], act.at[here, core, h], load_sem.at[h])
        for h in range(2)
    ]
    loads += [
        pltpu.make_async_copy(src, dst, load_sem.at[2 + i])
        for i, (src, dst) in enumerate(((kept_in, kept.at[tok]), (sgn_in, sgn), (scl_in, scl), (wg_in, wg), (wu_in, wu)))
    ]
    for load in loads:
        load.start()

    barrier = pltpu.get_barrier_semaphore()

    def greet_hid(i, carry):
        pl.semaphore_signal(barrier, inc=1, device_id={"hid": lax.rem(hid + i, hid_n)}, device_id_type=MESH)
        return carry

    def greet_tok(i, carry):
        pl.semaphore_signal(barrier, inc=1, device_id={"tok": lax.rem(tok + i, tok_n)}, device_id_type=MESH)
        return carry

    lax.fori_loop(1, hid_n, greet_hid, 0)
    lax.fori_loop(1, tok_n, greet_tok, 0)
    pl.semaphore_wait(barrier, hid_n + tok_n - 2)

    sends = []

    def send(ref, send_sem, recv_sem, device):
        copy = pltpu.make_async_remote_copy(
            src_ref=ref, dst_ref=ref, send_sem=send_sem, recv_sem=recv_sem, device_id=device, device_id_type=MESH
        )
        copy.start()
        sends.append(copy)

    def arrive(ref, send_sem, recv_sem):
        pltpu.make_async_remote_copy(
            src_ref=ref, dst_ref=ref, send_sem=send_sem, recv_sem=recv_sem, device_id=sibling, device_id_type=MESH
        ).wait_recv()

    def piece(item, d, c=None):
        return act.at[chip(item < 2, d), core if c is None else c, 0 if item in (0, 3) else 1]

    def slot(d):
        return d if d >= 0 else far - d

    def go_z(item, d):
        if 0 <= d < far:
            send(piece(item, d), zs.at[0, d, item], zr.at[0, d, item], ahead)
        if -(far - 1) < d <= 0:
            send(piece(item, d), zs.at[1, -d, item], zr.at[1, -d, item], behind)

    def from_z(item, d):
        if d > 0:
            arrive(piece(item, d), zs.at[0, d - 1, item], zr.at[0, d - 1, item])
        else:
            arrive(piece(item, d), zs.at[1, -d - 1, item], zr.at[1, -d - 1, item])

    def go_x(item, d):
        k = slot(d) if item == 0 else 2 * far
        send(piece(item, d), xs.at[k], xr.at[k], across)

    def from_x(item, d):
        k = slot(d) if item == 3 else 2 * far
        arrive(piece(item, d), xs.at[k], xr.at[k])

    def go_sibling(item, d):
        send(piece(item, d), ss.at[item, slot(d)], sr.at[item, slot(d)], sibling)

    def from_sibling(item, d):
        e = -d if abs(d) < far else d
        arrive(piece(item, d, 1 - core), ss.at[item, slot(e)], sr.at[item, slot(e)])

    def matmul(blocks, which, first=False):
        def tile(m, carry):
            rows = pl.ds(pl.multiple_of(m * rows_step, rows_step), rows_step)
            out_rows = pl.ds(pl.multiple_of(which * half + m * rows_step, rows_step), rows_step)
            left = jnp.concatenate([act[q, c, which, rows, :] for q in blocks for c in range(2)], axis=1)
            for weight, acc in ((wg, accg), (wu, accu)):
                right = jnp.concatenate(
                    [weight[pl.ds(pl.multiple_of(q * depth, depth), depth), :] for q in blocks], axis=0
                )
                product = jnp.dot(left, right, preferred_element_type=F32)
                acc[out_rows, :] = product if first else acc[out_rows, :] + product
            return carry

        lax.fori_loop(0, half // rows_step, tile, 0)

    def offsets(k):
        return [k] if k in (0, far) else [k, -k]

    def unit(items, which, first=False):
        for item, d in items:
            from_sibling(item, d)
        matmul([chip(item < 2, d) for item, d in items], which, first)

    for load in loads[:2]:
        load.wait()
    go_z(0, 0)
    go_x(1, 0)
    go_x(0, 0)
    go_z(1, 0)
    go_sibling(0, 0)
    go_sibling(1, 0)
    loads[2].wait()

    def send_kept(i, carry):
        pltpu.make_async_remote_copy(
            src_ref=kept.at[tok], dst_ref=kept.at[tok], send_sem=bulk_s.at[0], recv_sem=bulk_r.at[0],
            device_id={"tok": lax.rem(tok + i, tok_n)}, device_id_type=MESH,
        ).start()
        return carry

    lax.fori_loop(1, tok_n, send_kept, 0)

    def settle(ref, sem):
        pltpu.make_async_copy(ref, ref, sem).wait()

    from_x(2, 0)
    go_z(2, 0)
    go_sibling(2, 0)

    loads[3].wait()
    loads[4].wait()
    groups, lanes = sgn.shape
    factor = (2 * sgn[...] - 1).astype(F32) * scl[...]
    for g in range(groups):
        column = diagonal_column(factor[g : g + 1, :], lanes)
        fcol[g * lanes : (g + 1) * lanes, :] = jnp.broadcast_to(column, (lanes, fcol.shape[1]))

    loads[5].wait()
    loads[6].wait()

    def sign_rows(j, carry):
        owner = bit_parity(j & tok)
        column = diagonal_column(kept[j].astype(F32), kept_n).astype(jnp.int32)
        places = lax.broadcasted_iota(jnp.int32, (kept_n, tokens), 1)
        parity = bit_parity(jnp.broadcast_to(column, (kept_n, tokens)) & places) ^ owner
        table[pl.ds(pl.multiple_of(j * kept_n, kept_n), kept_n), :] = (1 - 2 * parity).astype(F32).astype(BF16)
        return carry

    for k in range(1, far + 1):
        near = offsets(k)
        before = offsets(k - 1)
        for d in near:
            from_z(0, d)
            go_z(0, d)
            go_x(0, d)
            go_sibling(0, d)
        if k == 1:
            unit([(0, 0)], 0, True)
        else:
            unit([(0, d) for d in before] + [(3, d) for d in offsets(k - 2)], 0)
        for d in near:
            from_z(1, d)
            go_z(1, d)
            go_sibling(1, d)
        for d in before:
            from_x(3, d)
            go_sibling(3, d)
        if k == 1:
            settle(kept.at[pl.ds(0, tok_n - 1)], bulk_s.at[0])
            settle(kept.at[pl.ds(0, tok_n - 1)], bulk_r.at[0])
            lax.fori_loop(0, tok_n, sign_rows, 0)
        for d in near:
            from_z(2, d)
            go_z(2, d)
            go_sibling(2, d)
        unit([(1, d) for d in before] + [(2, d) for d in before], 1, k == 1)
    from_x(3, far)
    go_sibling(3, far)
    unit([(0, far)] + [(3, d) for d in offsets(far - 1)], 0)
    unit([(1, far), (2, far)], 1)
    unit([(3, far)], 0)

    def activate(m, carry):
        rows = pl.ds(pl.multiple_of(m * 128, 128), 128)
        gate = accg[rows, :]
        silu = gate / (1.0 + jnp.exp(-gate))
        hidden[rows, :] = (fcol[rows, 0:1] * silu * accu[rows, :]).astype(BF16)
        return carry

    lax.fori_loop(0, tokens // 128, activate, 0)

    owners_step = max(tok_n // 2, 1)
    for b in range(tok_n // owners_step):
        rows = slice(b * owners_step * kept_n, (b + 1) * owners_step * kept_n)
        product = jnp.dot(table[rows, :], hidden[...], preferred_element_type=F32).astype(BF16)
        for i in range(owners_step):
            part[b * owners_step + i] = product[i * kept_n : (i + 1) * kept_n, :]

    def send_part(i, carry):
        peer = lax.rem(tok + i, tok_n)
        pltpu.make_async_remote_copy(
            src_ref=part.at[peer], dst_ref=got.at[tok], send_sem=bulk_s.at[1], recv_sem=bulk_r.at[1],
            device_id={"tok": peer}, device_id_type=MESH,
        ).start()
        return carry

    lax.fori_loop(1, tok_n, send_part, 0)
    got[tok] = part[tok]
    settle(got.at[pl.ds(0, tok_n - 1)], bulk_r.at[1])
    total = got[0].astype(F32)
    for j in range(1, tok_n):
        total = total + got[j].astype(F32)
    mine = (total * row_scale).astype(BF16)
    sk[tok] = mine

    def send_sketch(i, carry):
        pltpu.make_async_remote_copy(
            src_ref=sk.at[tok], dst_ref=sk.at[tok], send_sem=bulk_s.at[2], recv_sem=bulk_r.at[2],
            device_id={"tok": lax.rem(tok + i, tok_n)}, device_id_type=MESH,
        ).start()
        return carry

    lax.fori_loop(1, tok_n, send_sketch, 0)
    settle(sk.at[pl.ds(0, tok_n - 1)], bulk_r.at[2])
    every = sk[...].reshape(tok_n * kept_n, sk.shape[-1])
    gram = lax.dot_general(mine, every, (((1,), (1,)), ((), ())), preferred_element_type=F32) * gram_scale

    tile_rows, tile_lanes = gs.shape[1:]
    across_n = gram.shape[1] // tile_lanes
    for t in range(hid_n):
        a, b = divmod(t, across_n)
        gs[t] = gram[a * tile_rows : (a + 1) * tile_rows, b * tile_lanes : (b + 1) * tile_lanes]

    def send_tile(i, carry):
        peer = lax.rem(hid + i, hid_n)
        pltpu.make_async_remote_copy(
            src_ref=gs.at[peer], dst_ref=gr.at[hid], send_sem=bulk_s.at[3], recv_sem=bulk_r.at[3],
            device_id={"hid": peer}, device_id_type=MESH,
        ).start()
        return carry

    lax.fori_loop(1, hid_n, send_tile, 0)
    gr[hid] = gs[hid]
    settle(gr.at[pl.ds(0, hid_n - 1)], bulk_r.at[3])
    gf[hid] = jnp.sum(gr[...], axis=0)

    def send_sum(i, carry):
        pltpu.make_async_remote_copy(
            src_ref=gf.at[hid], dst_ref=gf.at[hid], send_sem=bulk_s.at[4], recv_sem=bulk_r.at[4],
            device_id={"hid": lax.rem(hid + i, hid_n)}, device_id_type=MESH,
        ).start()
        return carry

    lax.fori_loop(1, hid_n, send_sum, 0)
    for copy in sends:
        copy.wait_send()
    settle(part.at[pl.ds(0, tok_n - 1)], bulk_s.at[1])
    settle(sk.at[pl.ds(0, tok_n - 1)], bulk_s.at[2])
    settle(gs.at[pl.ds(0, hid_n - 1)], bulk_s.at[3])
    settle(gf.at[pl.ds(0, hid_n - 1)], bulk_r.at[4])
    for t in range(hid_n):
        a, b = divmod(t, across_n)
        out_ref[a * tile_rows : (a + 1) * tile_rows, b * tile_lanes : (b + 1) * tile_lanes] = gf[t]
    settle(gf.at[pl.ds(0, hid_n - 1)], bulk_s.at[4])


def per_device(tok_n, hid_n, activations, gate_weight, up_weight, row_signs, row_scales, kept_rows):
    tokens, width = activations.shape
    depth, units = gate_weight.shape
    kept_n = kept_rows.shape[0]
    zn = hid_n // 4
    far = zn // 2
    lanes = min(128, tokens)
    tile_lanes = kept_n * kept_n * tok_n // 8 // hid_n
    hbm = pl.BlockSpec(memory_space=pl.ANY)
    dma = pltpu.SemaphoreType.DMA
    return pl.pallas_call(
        functools.partial(fused, tok_n, hid_n, float(tokens * tok_n) ** -0.5, float(FF) ** -0.5),
        out_shape=jax.ShapeDtypeStruct((kept_n, kept_n * tok_n), F32),
        in_specs=[hbm] * 6,
        out_specs=pl.BlockSpec(memory_space=pltpu.VMEM),
        scratch_shapes=[
            pltpu.VMEM((hid_n // 2, 2, 2, tokens // 2, width), BF16),
            pltpu.VMEM((depth, units), BF16),
            pltpu.VMEM((depth, units), BF16),
            pltpu.VMEM((tokens, units), F32),
            pltpu.VMEM((tokens, units), F32),
            pltpu.VMEM((tokens, 128), F32),
            pltpu.VMEM((kept_n * tok_n, tokens), BF16),
            pltpu.VMEM((tokens, units), BF16),
            pltpu.VMEM((tokens // lanes, lanes), jnp.int32),
            pltpu.VMEM((tokens // lanes, lanes), F32),
            pltpu.VMEM((tok_n, 1, kept_n), jnp.int32),
            pltpu.VMEM((tok_n, kept_n, units), BF16),
            pltpu.VMEM((tok_n, kept_n, units), BF16),
            pltpu.VMEM((tok_n, kept_n, units), BF16),
            pltpu.VMEM((hid_n, 8, tile_lanes), F32),
            pltpu.VMEM((hid_n, 8, tile_lanes), F32),
            pltpu.VMEM((hid_n, 8, tile_lanes), F32),
            dma((7,)),
            dma((2, far, 3)),
            dma((2, far, 3)),
            dma((2 * far + 1,)),
            dma((2 * far + 1,)),
            dma((4, 2 * far)),
            dma((4, 2 * far)),
            dma((5,)),
            dma((5,)),
        ],
        compiler_params=pltpu.CompilerParams(
            collective_id=0, has_side_effects=True, vmem_limit_bytes=60 * 1024 * 1024
        ),
        name="sketch_gram",
    )(
        activations, gate_weight, up_weight,
        row_signs.reshape(-1, lanes), row_scales.reshape(-1, lanes), kept_rows.reshape(1, -1),
    )


def solution(mesh):
    placed = (P("tok", "hid"), P(None, "hid"), P(None, "hid"), P("tok"), P("tok"), P("tok"))
    return jax.shard_map(
        functools.partial(per_device, mesh.shape["tok"], mesh.shape["hid"]),
        mesh=mesh, in_specs=placed, out_specs=P("tok", None), check_vma=False,
    )
```

time: 199 us -> 93.2 us (0.47)
  waiting for transfers between devices: 86 us -> 0 us
  Pallas kernels: 0 us -> 78.4 us
  blocking collectives: 64.3 us -> 0 us
  matrix products: 22.8 us -> 0 us
  between operations: 13.5 us -> 0.01 us
  local copies, waits for them, and re-layouts: 3.06 us -> 14.5 us
  starting transfers between devices: 7.48 us -> 0 us
    all_gather x1 -> x0, waiting for transfers between devices: 79.6 us -> none  [per_device(): shard_cols = lax.all_gather(activations, 'hid', axis=1, tiled=True)]
    pallas_call x0 -> x1, Pallas kernels: none -> 78.4 us  [per_device(): pl.pallas_call(functools.partial(fused, tok_n, hid_n, float(tokens * tok_...]
    all_to_all x4 -> x0, blocking collectives: 64.3 us -> none  [the longest x2 38 us: summed_on_arrival(): tiles = lax.all_to_all(split_up(array, dim, peers), axis, 0, 0, tiled=True)]
    dot_general x3 -> x0, matrix products: 22.8 us -> none  [the longest x1 12.8 us: per_device(): jnp.dot(signs_table, signed_hidden, preferred_element_type=jnp.float32)]
    unnamed x0 -> x3, local copies, waits for them, and re-layouts: none -> 14.5 us
    all_to_all x1 -> x0, starting transfers between devices: 7.48 us -> none  [from_everyone(): return lax.all_to_all(copies, axis, split_axis=0, concat_axis=0, tiled=True)]
    all_to_all x1 -> x0, waiting for transfers between devices: 5.7 us -> none  [from_everyone(): return lax.all_to_all(copies, axis, split_axis=0, concat_axis=0, tiled=True)]
  transfers between devices with their start and end apart: 2 -> 0, of which waited for: 2 -> 0; matrix products, arithmetic and copies ran while one was open for 2% -> 0% of each run, Pallas kernels for 0% -> 0%
where the time goes in v1:
time: 93.2 us; the launch traced here: 92.9 us
  Pallas kernels  78.4 us (84%)
  local copies, waits for them, and re-layouts  14.5 us (16%)
    pallas_call x1, Pallas kernels, per_device(): pl.pallas_call(functools.partial(fused, tok_n, hid_n, float(tokens * tok_...  78.4 us
    unnamed x3, local copies, waits for them, and re-layouts  14.5 us

profile of v1, /device:TPU:1, one launch (start us, length us, event | category | flops | bytes accessed | tf_op | source)
XLA Modules:
  0.0 92.9 jit_solution(2506164604286203535)
XLA Ops:
  0.0 6.4 %copy.7.wg_in = bf16[4096,448]{1,0:T(8,128)(2,1)} copy(bf16[4096,448]{0,1:T(8,128)(2,1)} %param.7) | data formatting | bytes 7340032 | tf_op args[1]
  6.4 6.5 %copy.8.wu_in = bf16[4096,448]{1,0:T(8,128)(2,1)} copy(bf16[4096,448]{0,1:T(8,128)(2,1)} %param.8) | data formatting | bytes 7340032 | tf_op args[2]
  12.9 78.4 %sketch_gram.1 = f32[64,512]{1,0:T(8,128)} custom-call(bf16[1024,128]{1,0:T(8,128)(2,1)} %act_in.1, bf16[4096,448]{1,0:T(8,128)(2,1)} %copy.7.wg_in, bf16[4096,448]{1,0:T(8,128)(2,1)} %copy.8.wu_in, s32[8,128]{1,0:T(8,128)} %bitcast.3, f32[8,128]{1,0:T(8,128)} %bitcast.4, s32[1,64]{1,0:T(1,128)} %bitcast.5), custom_call_target="tpu_custom_call" | custom-call | tf_op jit(solution)/shard_map/sketch_gram/pallas_call | solution.py:332
  91.3 1.6 %copy.10 = f32[64,512]{1,0:T(8,128)} copy(f32[64,512]{1,0:T(8,128)} %sketch_gram.1) | data formatting | bytes 262144

commit v2 on v1

--- a/solution.py
+++ b/solution.py
@@ -30,7 +30,7 @@
 def fused(
     tok_n, hid_n, row_scale, gram_scale,
     act_in, wg_in, wu_in, sgn_in, scl_in, kept_in, out_ref,
-    act, wg, wu, accg, accu, fcol, table, hidden, sgn, scl, kept,
+    act, weights, acc, table, hidden, sgn, scl, kept,
     part, got, sk, gs, gr, gf,
     load_sem, zs, zr, xs, xr, ss, sr, bulk_s, bulk_r,
 ):
@@ -41,6 +41,7 @@
     rows_step = min(ROWS_STEP, half)
     depth = 2 * width
     kept_n = kept.shape[-1]
+    units = wg_in.shape[0]
     tok = lax.axis_index("tok")
     hid = lax.axis_index("hid")
     core = lax.rem(hid, 2)
@@ -67,7 +68,8 @@
     ]
     loads += [
         pltpu.make_async_copy(src, dst, load_sem.at[2 + i])
-        for i, (src, dst) in enumerate(((kept_in, kept.at[tok]), (sgn_in, sgn), (scl_in, scl), (wg_in, wg), (wu_in, wu)))
+        for i, (src, dst) in enumerate(((kept_in, kept.at[tok]), (sgn_in, sgn), (scl_in, scl),
+                                         (wg_in, weights.at[pl.ds(0, units), :]), (wu_in, weights.at[pl.ds(units, units), :])))
     ]
     for load in loads:
         load.start()
@@ -136,14 +138,13 @@
     def matmul(blocks, which, first=False):
         def tile(m, carry):
             rows = pl.ds(pl.multiple_of(m * rows_step, rows_step), rows_step)
-            out_rows = pl.ds(pl.multiple_of(which * half + m * rows_step, rows_step), rows_step)
-            left = jnp.concatenate([act[q, c, which, rows, :] for q in blocks for c in range(2)], axis=1)
-            for weight, acc in ((wg, accg), (wu, accu)):
-                right = jnp.concatenate(
-                    [weight[pl.ds(pl.multiple_of(q * depth, depth), depth), :] for q in blocks], axis=0
-                )
-                product = jnp.dot(left, right, preferred_element_type=F32)
-                acc[out_rows, :] = product if first else acc[out_rows, :] + product
+            columns = pl.ds(pl.multiple_of(which * half + m * rows_step, rows_step), rows_step)
+            left = jnp.concatenate(
+                [weights[:, pl.ds(pl.multiple_of(q * depth, depth), depth)] for q in blocks], axis=1
+            )
+            right = jnp.concatenate([act[q, c, which, rows, :] for q in blocks for c in range(2)], axis=1)
+            product = lax.dot_general(left, right, (((1,), (1,)), ((), ())), preferred_element_type=F32)
+            acc[:, columns] = product if first else acc[:, columns] + product
             return carry
 
         lax.fori_loop(0, half // rows_step, tile, 0)
@@ -184,12 +185,6 @@
 
     loads[3].wait()
     loads[4].wait()
-    groups, lanes = sgn.shape
-    factor = (2 * sgn[...] - 1).astype(F32) * scl[...]
-    for g in range(groups):
-        column = diagonal_column(factor[g : g + 1, :], lanes)
-        fcol[g * lanes : (g + 1) * lanes, :] = jnp.broadcast_to(column, (lanes, fcol.shape[1]))
-
     loads[5].wait()
     loads[6].wait()
 
@@ -236,18 +231,21 @@
     unit([(3, far)], 0)
 
     def activate(m, carry):
-        rows = pl.ds(pl.multiple_of(m * 128, 128), 128)
-        gate = accg[rows, :]
+        gate = acc[pl.ds(pl.multiple_of(m * 64, 64), 64), :]
+        up = acc[pl.ds(pl.multiple_of(units + m * 64, 64), 64), :]
+        factor = (2 * sgn[...] - 1).astype(F32) * scl[...]
         silu = gate / (1.0 + jnp.exp(-gate))
-        hidden[rows, :] = (fcol[rows, 0:1] * silu * accu[rows, :]).astype(BF16)
-        return carry
-
-    lax.fori_loop(0, tokens // 128, activate, 0)
+        hidden[pl.ds(pl.multiple_of(m * 64, 64), 64), :] = (factor * silu * up).astype(BF16)
+        return carry
+
+    lax.fori_loop(0, units // 64, activate, 0)
 
     owners_step = max(tok_n // 2, 1)
     for b in range(tok_n // owners_step):
         rows = slice(b * owners_step * kept_n, (b + 1) * owners_step * kept_n)
-        product = jnp.dot(table[rows, :], hidden[...], preferred_element_type=F32).astype(BF16)
+        product = lax.dot_general(
+            table[rows, :], hidden[...], (((1,), (1,)), ((), ())), preferred_element_type=F32
+        ).astype(BF16)
         for i in range(owners_step):
             part[b * owners_step + i] = product[i * kept_n : (i + 1) * kept_n, :]
 
@@ -325,7 +323,6 @@
     kept_n = kept_rows.shape[0]
     zn = hid_n // 4
     far = zn // 2
-    lanes = min(128, tokens)
     tile_lanes = kept_n * kept_n * tok_n // 8 // hid_n
     hbm = pl.BlockSpec(memory_space=pl.ANY)
     dma = pltpu.SemaphoreType.DMA
@@ -336,15 +333,12 @@
         out_specs=pl.BlockSpec(memory_space=pltpu.VMEM),
         scratch_shapes=[
             pltpu.VMEM((hid_n // 2, 2, 2, tokens // 2, width), BF16),
-            pltpu.VMEM((depth, units), BF16),
-            pltpu.VMEM((depth, units), BF16),
-            pltpu.VMEM((tokens, units), F32),
-            pltpu.VMEM((tokens, units), F32),
-            pltpu.VMEM((tokens, 128), F32),
+            pltpu.VMEM((2 * units, depth), BF16),
+            pltpu.VMEM((2 * units, tokens), F32),
             pltpu.VMEM((kept_n * tok_n, tokens), BF16),
-            pltpu.VMEM((tokens, units), BF16),
-            pltpu.VMEM((tokens // lanes, lanes), jnp.int32),
-            pltpu.VMEM((tokens // lanes, lanes), F32),
+            pltpu.VMEM((units, tokens), BF16),
+            pltpu.VMEM((1, tokens), jnp.int32),
+            pltpu.VMEM((1, tokens), F32),
             pltpu.VMEM((tok_n, 1, kept_n), jnp.int32),
             pltpu.VMEM((tok_n, kept_n, units), BF16),
             pltpu.VMEM((tok_n, kept_n, units), BF16),
@@ -367,8 +361,8 @@
         ),
         name="sketch_gram",
     )(
-        activations, gate_weight, up_weight,
-        row_signs.reshape(-1, lanes), row_scales.reshape(-1, lanes), kept_rows.reshape(1, -1),
+        activations, gate_weight.T, up_weight.T,
+        row_signs.reshape(1, -1), row_scales.reshape(1, -1), kept_rows.reshape(1, -1),
     )
 
 

time: 93.2 us -> 79.9 us (0.86)
  local copies, waits for them, and re-layouts: 14.5 us -> 1.57 us
    unnamed x3 -> x1, local copies, waits for them, and re-layouts: 14.5 us -> 1.57 us
where the time goes in v2:
time: 79.9 us; the launch traced here: 79.8 us
  Pallas kernels  78.2 us (98%)
  local copies, waits for them, and re-layouts  1.57 us (2%)
    pallas_call x1, Pallas kernels, per_device(): pl.pallas_call(functools.partial(fused, tok_n, hid_n, float(tokens * tok_...  78.2 us

profile of v2, /device:TPU:1, one launch (start us, length us, event | category | flops | bytes accessed | tf_op | source)
XLA Modules:
  0.0 79.8 jit_solution(5925898909958623309)
XLA Ops:
  0.0 78.2 %sketch_gram.1 = f32[64,512]{1,0:T(8,128)} custom-call(bf16[1024,128]{1,0:T(8,128)(2,1)} %act_in.1, bf16[448,4096]{1,0:T(8,128)(2,1)} %bitcast.5, bf16[448,4096]{1,0:T(8,128)(2,1)} %bitcast.6, s32[1,1024]{1,0:T(1,128)} %bitcast.7, f32[1,1024]{1,0:T(1,128)} %bitcast.8, s32[1,64]{1,0:T(1,128)} %bitcast.9), custom_call_target="tpu_custom_call" | custom-call | tf_op jit(solution)/shard_map/sketch_gram/pallas_call | solution.py:329
  78.2 1.6 %copy.8 = f32[64,512]{1,0:T(8,128)} copy(f32[64,512]{1,0:T(8,128)} %sketch_gram.1) | data formatting | bytes 262144

commit v3 on v2

--- a/solution.py
+++ b/solution.py
@@ -76,17 +76,14 @@
 
     barrier = pltpu.get_barrier_semaphore()
 
-    def greet_hid(i, carry):
-        pl.semaphore_signal(barrier, inc=1, device_id={"hid": lax.rem(hid + i, hid_n)}, device_id_type=MESH)
-        return carry
-
-    def greet_tok(i, carry):
+    def greet(i, carry):
         pl.semaphore_signal(barrier, inc=1, device_id={"tok": lax.rem(tok + i, tok_n)}, device_id_type=MESH)
         return carry
 
-    lax.fori_loop(1, hid_n, greet_hid, 0)
-    lax.fori_loop(1, tok_n, greet_tok, 0)
-    pl.semaphore_wait(barrier, hid_n + tok_n - 2)
+    for neighbour in (ahead, behind, across, sibling):
+        pl.semaphore_signal(barrier, inc=1, device_id=neighbour, device_id_type=MESH)
+    lax.fori_loop(1, tok_n, greet, 0)
+    pl.semaphore_wait(barrier, 4 + tok_n - 1)
 
     sends = []
 
@@ -161,8 +158,8 @@
         load.wait()
     go_z(0, 0)
     go_x(1, 0)
+    go_z(1, 0)
     go_x(0, 0)
-    go_z(1, 0)
     go_sibling(0, 0)
     go_sibling(1, 0)
     loads[2].wait()
@@ -178,15 +175,6 @@
 
     def settle(ref, sem):
         pltpu.make_async_copy(ref, ref, sem).wait()
-
-    from_x(2, 0)
-    go_z(2, 0)
-    go_sibling(2, 0)
-
-    loads[3].wait()
-    loads[4].wait()
-    loads[5].wait()
-    loads[6].wait()
 
     def sign_rows(j, carry):
         owner = bit_parity(j & tok)
@@ -196,39 +184,46 @@
         table[pl.ds(pl.multiple_of(j * kept_n, kept_n), kept_n), :] = (1 - 2 * parity).astype(F32).astype(BF16)
         return carry
 
-    for k in range(1, far + 1):
-        near = offsets(k)
-        before = offsets(k - 1)
-        for d in near:
-            from_z(0, d)
-            go_z(0, d)
-            go_x(0, d)
-            go_sibling(0, d)
-        if k == 1:
-            unit([(0, 0)], 0, True)
-        else:
-            unit([(0, d) for d in before] + [(3, d) for d in offsets(k - 2)], 0)
-        for d in near:
-            from_z(1, d)
-            go_z(1, d)
-            go_sibling(1, d)
-        for d in before:
-            from_x(3, d)
-            go_sibling(3, d)
+    def ring(r):
+        return [(1 + (r + 1) % 2, d) for d in offsets((r + 1) // 2)]
+
+    for k in range(1, 2 * far + 1):
+        if k <= far:
+            for d in offsets(k):
+                from_z(0, d)
+                go_z(0, d)
+                go_x(0, d)
+                go_sibling(0, d)
+            if k == 1:
+                from_x(2, 0)
+                go_sibling(2, 0)
+                go_z(2, 0)
+            else:
+                for item, d in ring(k - 1):
+                    go_z(item, d)
+        for item, d in ring(k):
+            from_z(item, d)
+            if k >= far:
+                go_z(item, d)
+            go_sibling(item, d)
+        if k <= far + 1:
+            for d in offsets(k - 1):
+                from_x(3, d)
+                go_sibling(3, d)
         if k == 1:
             settle(kept.at[pl.ds(0, tok_n - 1)], bulk_s.at[0])
             settle(kept.at[pl.ds(0, tok_n - 1)], bulk_r.at[0])
             lax.fori_loop(0, tok_n, sign_rows, 0)
-        for d in near:
-            from_z(2, d)
-            go_z(2, d)
-            go_sibling(2, d)
-        unit([(1, d) for d in before] + [(2, d) for d in before], 1, k == 1)
-    from_x(3, far)
-    go_sibling(3, far)
-    unit([(0, far)] + [(3, d) for d in offsets(far - 1)], 0)
-    unit([(1, far), (2, far)], 1)
-    unit([(3, far)], 0)
+            for load in loads[3:]:
+                load.wait()
+            unit([(0, 0), (0, 1), (0, -1)], 0, True)
+        elif k <= far + 2:
+            unit(([(0, d) for d in offsets(k)] if k <= far else []) + [(3, d) for d in offsets(k - 2)], 0)
+        if k == 2:
+            unit([(1, 0), (2, 0)] + ring(1), 1, True)
+        elif k % 2 == 0:
+            unit(ring(k - 2) + (ring(k - 1) if k < 2 * far else []), 1)
+    unit(ring(2 * far - 1) + ring(2 * far), 1)
 
     def activate(m, carry):
         gate = acc[pl.ds(pl.multiple_of(m * 64, 64), 64), :]
@@ -240,14 +235,26 @@
 
     lax.fori_loop(0, units // 64, activate, 0)
 
+    strips = units // 128
+
+    def packed(rows):
+        tail = rows[:, strips * 128 :]
+        tail = jnp.concatenate([tail[: kept_n // 2], tail[kept_n // 2 :]], axis=1)
+        return jnp.concatenate([rows[:, c * 128 : (c + 1) * 128] for c in range(strips)] + [tail], axis=0)
+
+    def unpacked(strip):
+        blocks = [strip[c * kept_n : (c + 1) * kept_n, :] for c in range(strips)]
+        tail = strip[strips * kept_n :, :]
+        return jnp.concatenate(blocks + [jnp.concatenate([tail[:, :64], tail[:, 64:]], axis=0)], axis=1)
+
     owners_step = max(tok_n // 2, 1)
     for b in range(tok_n // owners_step):
         rows = slice(b * owners_step * kept_n, (b + 1) * owners_step * kept_n)
         product = lax.dot_general(
             table[rows, :], hidden[...], (((1,), (1,)), ((), ())), preferred_element_type=F32
-        ).astype(BF16)
+        )
         for i in range(owners_step):
-            part[b * owners_step + i] = product[i * kept_n : (i + 1) * kept_n, :]
+            part[b * owners_step + i] = packed(product[i * kept_n : (i + 1) * kept_n, :]).astype(BF16)
 
     def send_part(i, carry):
         peer = lax.rem(tok + i, tok_n)
@@ -275,8 +282,8 @@
 
     lax.fori_loop(1, tok_n, send_sketch, 0)
     settle(sk.at[pl.ds(0, tok_n - 1)], bulk_r.at[2])
-    every = sk[...].reshape(tok_n * kept_n, sk.shape[-1])
-    gram = lax.dot_general(mine, every, (((1,), (1,)), ((), ())), preferred_element_type=F32) * gram_scale
+    every = jnp.concatenate([unpacked(sk[j].astype(F32)).astype(BF16) for j in range(tok_n)], axis=0)
+    gram = lax.dot_general(unpacked(mine.astype(F32)).astype(BF16), every, (((1,), (1,)), ((), ())), preferred_element_type=F32) * gram_scale
 
     tile_rows, tile_lanes = gs.shape[1:]
     across_n = gram.shape[1] // tile_lanes
@@ -340,9 +347,9 @@
             pltpu.VMEM((1, tokens), jnp.int32),
             pltpu.VMEM((1, tokens), F32),
             pltpu.VMEM((tok_n, 1, kept_n), jnp.int32),
-            pltpu.VMEM((tok_n, kept_n, units), BF16),
-            pltpu.VMEM((tok_n, kept_n, units), BF16),
-            pltpu.VMEM((tok_n, kept_n, units), BF16),
+            pltpu.VMEM((tok_n, kept_n * units // 128, 128), BF16),
+            pltpu.VMEM((tok_n, kept_n * units // 128, 128), BF16),
+            pltpu.VMEM((tok_n, kept_n * units // 128, 128), BF16),
             pltpu.VMEM((hid_n, 8, tile_lanes), F32),
             pltpu.VMEM((hid_n, 8, tile_lanes), F32),
             pltpu.VMEM((hid_n, 8, tile_lanes), F32),

time: 79.9 us -> 80 us (level)
  no operation moved by 1% of the time
where the time goes in v3:
time: 80 us; the launch traced here: 79.9 us
  Pallas kernels  78.3 us (98%)
  local copies, waits for them, and re-layouts  1.57 us (2%)
    pallas_call x1, Pallas kernels, per_device(): pl.pallas_call(functools.partial(fused, tok_n, hid_n, float(tokens * tok_...  78.3 us

profile of v3, /device:TPU:1, one launch (start us, length us, event | category | flops | bytes accessed | tf_op | source)
XLA Modules:
  0.0 79.9 jit_solution(13855064374926468038)
XLA Ops:
  0.0 78.3 %sketch_gram.1 = f32[64,512]{1,0:T(8,128)} custom-call(bf16[1024,128]{1,0:T(8,128)(2,1)} %act_in.1, bf16[448,4096]{1,0:T(8,128)(2,1)} %bitcast.5, bf16[448,4096]{1,0:T(8,128)(2,1)} %bitcast.6, s32[1,1024]{1,0:T(1,128)} %bitcast.7, f32[1,1024]{1,0:T(1,128)} %bitcast.8, s32[1,64]{1,0:T(1,128)} %bitcast.9), custom_call_target="tpu_custom_call" | custom-call | tf_op jit(solution)/shard_map/sketch_gram/pallas_call | solution.py:336
  78.3 1.6 %copy.8 = f32[64,512]{1,0:T(8,128)} copy(f32[64,512]{1,0:T(8,128)} %sketch_gram.1) | data formatting | bytes 262144

commit v4 on v3

--- a/solution.py
+++ b/solution.py
@@ -62,6 +62,19 @@
     across = at_hid(chip(False, 0))
     sibling = {"hid": here * 2 + 1 - core}
 
+    def ring_order(n):
+        return sorted(range(n), key=lambda step: -min(step, n - step))
+
+    hid_peers = [
+        (lax.rem(col + a, 2) * zn + lax.rem(z + step, zn)) * 2 + lax.rem(core + c, 2)
+        for step in ring_order(zn) for a in (1, 0) for c in (1, 0) if step or a or c
+    ]
+    yn = tok_n // 2
+    tok_peers = [
+        lax.rem(lax.div(tok, 2) + step, yn) * 2 + lax.rem(tok + a, 2)
+        for a in (1, 0) for step in ring_order(yn) if step or a
+    ]
+
     loads = [
         pltpu.make_async_copy(act_in.at[pl.ds(h * half, half), :], act.at[here, core, h], load_sem.at[h])
         for h in range(2)
@@ -76,13 +89,11 @@
 
     barrier = pltpu.get_barrier_semaphore()
 
-    def greet(i, carry):
-        pl.semaphore_signal(barrier, inc=1, device_id={"tok": lax.rem(tok + i, tok_n)}, device_id_type=MESH)
-        return carry
+    for peer in tok_peers:
+        pl.semaphore_signal(barrier, inc=1, device_id={"tok": peer}, device_id_type=MESH)
 
     for neighbour in (ahead, behind, across, sibling):
         pl.semaphore_signal(barrier, inc=1, device_id=neighbour, device_id_type=MESH)
-    lax.fori_loop(1, tok_n, greet, 0)
     pl.semaphore_wait(barrier, 4 + tok_n - 1)
 
     sends = []
@@ -164,14 +175,11 @@
     go_sibling(1, 0)
     loads[2].wait()
 
-    def send_kept(i, carry):
+    for peer in tok_peers:
         pltpu.make_async_remote_copy(
             src_ref=kept.at[tok], dst_ref=kept.at[tok], send_sem=bulk_s.at[0], recv_sem=bulk_r.at[0],
-            device_id={"tok": lax.rem(tok + i, tok_n)}, device_id_type=MESH,
-        ).start()
-        return carry
-
-    lax.fori_loop(1, tok_n, send_kept, 0)
+            device_id={"tok": peer}, device_id_type=MESH,
+        ).start()
 
     def settle(ref, sem):
         pltpu.make_async_copy(ref, ref, sem).wait()
@@ -256,15 +264,11 @@
         for i in range(owners_step):
             part[b * owners_step + i] = packed(product[i * kept_n : (i + 1) * kept_n, :]).astype(BF16)
 
-    def send_part(i, carry):
-        peer = lax.rem(tok + i, tok_n)
+    for peer in tok_peers:
         pltpu.make_async_remote_copy(
             src_ref=part.at[peer], dst_ref=got.at[tok], send_sem=bulk_s.at[1], recv_sem=bulk_r.at[1],
             device_id={"tok": peer}, device_id_type=MESH,
         ).start()
-        return carry
-
-    lax.fori_loop(1, tok_n, send_part, 0)
     got[tok] = part[tok]
     settle(got.at[pl.ds(0, tok_n - 1)], bulk_r.at[1])
     total = got[0].astype(F32)
@@ -273,14 +277,11 @@
     mine = (total * row_scale).astype(BF16)
     sk[tok] = mine
 
-    def send_sketch(i, carry):
+    for peer in tok_peers:
         pltpu.make_async_remote_copy(
             src_ref=sk.at[tok], dst_ref=sk.at[tok], send_sem=bulk_s.at[2], recv_sem=bulk_r.at[2],
-            device_id={"tok": lax.rem(tok + i, tok_n)}, device_id_type=MESH,
-        ).start()
-        return carry
-
-    lax.fori_loop(1, tok_n, send_sketch, 0)
+            device_id={"tok": peer}, device_id_type=MESH,
+        ).start()
     settle(sk.at[pl.ds(0, tok_n - 1)], bulk_r.at[2])
     every = jnp.concatenate([unpacked(sk[j].astype(F32)).astype(BF16) for j in range(tok_n)], axis=0)
     gram = lax.dot_general(unpacked(mine.astype(F32)).astype(BF16), every, (((1,), (1,)), ((), ())), preferred_element_type=F32) * gram_scale
@@ -291,27 +292,20 @@
         a, b = divmod(t, across_n)
         gs[t] = gram[a * tile_rows : (a + 1) * tile_rows, b * tile_lanes : (b + 1) * tile_lanes]
 
-    def send_tile(i, carry):
-        peer = lax.rem(hid + i, hid_n)
+    for peer in hid_peers:
         pltpu.make_async_remote_copy(
             src_ref=gs.at[peer], dst_ref=gr.at[hid], send_sem=bulk_s.at[3], recv_sem=bulk_r.at[3],
             device_id={"hid": peer}, device_id_type=MESH,
         ).start()
-        return carry
-
-    lax.fori_loop(1, hid_n, send_tile, 0)
     gr[hid] = gs[hid]
     settle(gr.at[pl.ds(0, hid_n - 1)], bulk_r.at[3])
     gf[hid] = jnp.sum(gr[...], axis=0)
 
-    def send_sum(i, carry):
+    for peer in hid_peers:
         pltpu.make_async_remote_copy(
             src_ref=gf.at[hid], dst_ref=gf.at[hid], send_sem=bulk_s.at[4], recv_sem=bulk_r.at[4],
-            device_id={"hid": lax.rem(hid + i, hid_n)}, device_id_type=MESH,
-        ).start()
-        return carry
-
-    lax.fori_loop(1, hid_n, send_sum, 0)
+            device_id={"hid": peer}, device_id_type=MESH,
+        ).start()
     for copy in sends:
         copy.wait_send()
     settle(part.at[pl.ds(0, tok_n - 1)], bulk_s.at[1])

time: 80 us -> 78 us (0.975)
  Pallas kernels: 78.3 us -> 76.4 us
    pallas_call x1, Pallas kernels: 78.3 us -> 76.4 us  [per_device(): pl.pallas_call(functools.partial(fused, tok_n, hid_n, float(tokens * tok_...]
where the time goes in v4:
time: 78 us; the launch traced here: 77.9 us
  Pallas kernels  76.4 us (98%)
  local copies, waits for them, and re-layouts  1.57 us (2%)
    pallas_call x1, Pallas kernels, per_device(): pl.pallas_call(functools.partial(fused, tok_n, hid_n, float(tokens * tok_...  76.4 us
    unnamed x1, local copies, waits for them, and re-layouts  1.57 us

profile of v4, /device:TPU:1, one launch (start us, length us, event | category | flops | bytes accessed | tf_op | source)
XLA Modules:
  0.0 77.9 jit_solution(15329319298120501720)
XLA Ops:
  0.0 76.4 %sketch_gram.1 = f32[64,512]{1,0:T(8,128)} custom-call(bf16[1024,128]{1,0:T(8,128)(2,1)} %act_in.1, bf16[448,4096]{1,0:T(8,128)(2,1)} %bitcast.5, bf16[448,4096]{1,0:T(8,128)(2,1)} %bitcast.6, s32[1,1024]{1,0:T(1,128)} %bitcast.7, f32[1,1024]{1,0:T(1,128)} %bitcast.8, s32[1,64]{1,0:T(1,128)} %bitcast.9), custom_call_target="tpu_custom_call" | custom-call | tf_op jit(solution)/shard_map/sketch_gram/pallas_call | solution.py:330
  76.4 1.6 %copy.8 = f32[64,512]{1,0:T(8,128)} copy(f32[64,512]{1,0:T(8,128)} %sketch_gram.1) | data formatting | bytes 262144

commit v5 on v4

--- a/solution.py
+++ b/solution.py
@@ -11,7 +11,6 @@
 MESH = pl.DeviceIdType.MESH
 F32 = jnp.float32
 BF16 = jnp.bfloat16
-ROWS_STEP = 256
 
 
 def bit_parity(value):
@@ -30,15 +29,14 @@
 def fused(
     tok_n, hid_n, row_scale, gram_scale,
     act_in, wg_in, wu_in, sgn_in, scl_in, kept_in, out_ref,
-    act, weights, acc, table, hidden, sgn, scl, kept,
+    act, guest, weights, acc, table, hidden, sgn, scl, factor, kept,
     part, got, sk, gs, gr, gf,
-    load_sem, zs, zr, xs, xr, ss, sr, bulk_s, bulk_r,
+    load_sem, zs, zr, xs, xr, cs, cr, ss, sr, bulk_s, bulk_r,
 ):
     zn = hid_n // 4
     far = zn // 2
     tokens, width = act_in.shape
-    half = tokens // 2
-    rows_step = min(ROWS_STEP, half)
+    block = tokens // 4
     depth = 2 * width
     kept_n = kept.shape[-1]
     units = wg_in.shape[0]
@@ -61,6 +59,10 @@
     behind = at_hid(chip(True, 1))
     across = at_hid(chip(False, 0))
     sibling = {"hid": here * 2 + 1 - core}
+    other_tok = tok + 1 - 2 * lax.rem(tok, 2)
+    cross = {"tok": other_tok, "hid": chip(False, 0) * 2 + core}
+    keep = 2 * col
+    give = 2 - 2 * col
 
     def ring_order(n):
         return sorted(range(n), key=lambda step: -min(step, n - step))
@@ -76,11 +78,11 @@
     ]
 
     loads = [
-        pltpu.make_async_copy(act_in.at[pl.ds(h * half, half), :], act.at[here, core, h], load_sem.at[h])
-        for h in range(2)
+        pltpu.make_async_copy(act_in.at[pl.ds(b * block, block), :], act.at[here, core, b], load_sem.at[b])
+        for b in range(4)
     ]
     loads += [
-        pltpu.make_async_copy(src, dst, load_sem.at[2 + i])
+        pltpu.make_async_copy(src, dst, load_sem.at[4 + i])
         for i, (src, dst) in enumerate(((kept_in, kept.at[tok]), (sgn_in, sgn), (scl_in, scl),
                                          (wg_in, weights.at[pl.ds(0, units), :]), (wu_in, weights.at[pl.ds(units, units), :])))
     ]
@@ -92,15 +94,16 @@
     for peer in tok_peers:
         pl.semaphore_signal(barrier, inc=1, device_id={"tok": peer}, device_id_type=MESH)
 
-    for neighbour in (ahead, behind, across, sibling):
+    for neighbour in (ahead, behind, across, sibling, cross):
         pl.semaphore_signal(barrier, inc=1, device_id=neighbour, device_id_type=MESH)
-    pl.semaphore_wait(barrier, 4 + tok_n - 1)
+    pl.semaphore_wait(barrier, 5 + tok_n - 1)
 
     sends = []
 
-    def send(ref, send_sem, recv_sem, device):
+    def send(ref, send_sem, recv_sem, device, there=None):
         copy = pltpu.make_async_remote_copy(
-            src_ref=ref, dst_ref=ref, send_sem=send_sem, recv_sem=recv_sem, device_id=device, device_id_type=MESH
+            src_ref=ref, dst_ref=ref if there is None else there, send_sem=send_sem, recv_sem=recv_sem,
+            device_id=device, device_id_type=MESH,
         )
         copy.start()
         sends.append(copy)
@@ -110,84 +113,118 @@
             src_ref=ref, dst_ref=ref, send_sem=send_sem, recv_sem=recv_sem, device_id=sibling, device_id_type=MESH
         ).wait_recv()
 
-    def piece(item, d, c=None):
-        return act.at[chip(item < 2, d), core if c is None else c, 0 if item in (0, 3) else 1]
-
     def slot(d):
         return d if d >= 0 else far - d
 
+    def z_piece(item, d):
+        shard = act.at[chip(item < 2, d), core]
+        return shard.at[pl.ds(0, 3)] if item == 0 else shard.at[3]
+
     def go_z(item, d):
         if 0 <= d < far:
-            send(piece(item, d), zs.at[0, d, item], zr.at[0, d, item], ahead)
+            send(z_piece(item, d), zs.at[0, d, item], zr.at[0, d, item], ahead)
         if -(far - 1) < d <= 0:
-            send(piece(item, d), zs.at[1, -d, item], zr.at[1, -d, item], behind)
+            send(z_piece(item, d), zs.at[1, -d, item], zr.at[1, -d, item], behind)
 
     def from_z(item, d):
-        if d > 0:
-            arrive(piece(item, d), zs.at[0, d - 1, item], zr.at[0, d - 1, item])
-        else:
-            arrive(piece(item, d), zs.at[1, -d - 1, item], zr.at[1, -d - 1, item])
-
-    def go_x(item, d):
-        k = slot(d) if item == 0 else 2 * far
-        send(piece(item, d), xs.at[k], xr.at[k], across)
-
-    def from_x(item, d):
-        k = slot(d) if item == 3 else 2 * far
-        arrive(piece(item, d), xs.at[k], xr.at[k])
+        way_in = (0, d - 1) if d > 0 else (1, -d - 1)
+        arrive(z_piece(item, d), zs.at[*way_in, item], zr.at[*way_in, item])
+
+    def go_x(kind, d):
+        b = (give, 1, 3)[kind]
+        send(act.at[chip(True, d), core, b], xs.at[kind, slot(d)], xr.at[kind, slot(d)], across)
+
+    def from_x(kind, d):
+        b = (keep, 1, 3)[kind]
+        arrive(act.at[chip(False, d), core, b], xs.at[kind, slot(d)], xr.at[kind, slot(d)])
+
+    def go_cross(kind, d):
+        q = chip(kind == 0, d)
+        send(act.at[q, core, keep], cs.at[kind, slot(d)], cr.at[kind, slot(d)], cross, guest.at[q, core])
+
+    def from_cross(kind, d):
+        arrive(guest.at[chip(kind == 1, d), core], cs.at[kind, slot(d)], cr.at[kind, slot(d)])
+
+    def shared(item, d, c):
+        if item >= 5:
+            return guest.at[chip(item == 6, d), c]
+        shard = act.at[chip(item < 2, d), c]
+        if item == 0:
+            return shard.at[pl.ds(col, 2)]
+        return shard.at[(None, 3, 3, keep, 1)[item]]
 
     def go_sibling(item, d):
-        send(piece(item, d), ss.at[item, slot(d)], sr.at[item, slot(d)], sibling)
+        send(shared(item, d, core), ss.at[item, slot(d)], sr.at[item, slot(d)], sibling)
 
     def from_sibling(item, d):
         e = -d if abs(d) < far else d
-        arrive(piece(item, d, 1 - core), ss.at[item, slot(e)], sr.at[item, slot(e)])
-
-    def matmul(blocks, which, first=False):
-        def tile(m, carry):
-            rows = pl.ds(pl.multiple_of(m * rows_step, rows_step), rows_step)
-            columns = pl.ds(pl.multiple_of(which * half + m * rows_step, rows_step), rows_step)
-            left = jnp.concatenate(
-                [weights[:, pl.ds(pl.multiple_of(q * depth, depth), depth)] for q in blocks], axis=1
-            )
-            right = jnp.concatenate([act[q, c, which, rows, :] for q in blocks for c in range(2)], axis=1)
-            product = lax.dot_general(left, right, (((1,), (1,)), ((), ())), preferred_element_type=F32)
-            acc[:, columns] = product if first else acc[:, columns] + product
-            return carry
-
-        lax.fori_loop(0, half // rows_step, tile, 0)
+        arrive(shared(item, d, 1 - core), ss.at[item, slot(e)], sr.at[item, slot(e)])
 
     def offsets(k):
         return [k] if k in (0, far) else [k, -k]
 
-    def unit(items, which, first=False):
+    def multiply(shards, read, start, first):
+        left = jnp.concatenate(
+            [weights[:, pl.ds(pl.multiple_of(q * depth, depth), depth)] for q in shards], axis=1
+        )
+        right = jnp.concatenate([read(q, c) for q in shards for c in range(2)], axis=1)
+        product = lax.dot_general(left, right, (((1,), (1,)), ((), ())), preferred_element_type=F32)
+        columns = pl.ds(start, block)
+        acc[:, columns] = product if first else acc[:, columns] + product
+
+    started = set()
+
+    def unit(group, items):
         for item, d in items:
-            from_sibling(item, d)
-        matmul([chip(item < 2, d) for item, d in items], which, first)
-
-    for load in loads[:2]:
+            for part_item in (3, 4) if item == 3 else (item,):
+                from_sibling(part_item, d)
+        shards = [chip(item in (0, 1, 6), d) for item, d in items]
+        first = group not in started
+        started.add(group)
+        if group == "main":
+            def tile(m, carry):
+                multiply(shards, lambda q, c: act[q, c, col + m], pl.multiple_of(m * block, block), first)
+                return carry
+
+            lax.fori_loop(0, 2, tile, 0)
+        elif group == "near":
+            multiply(shards, lambda q, c: act[q, c, 3], 2 * block, first)
+        else:
+            multiply(shards, lambda q, c: guest[q, c], 3 * block, first)
+
+    def settle(ref, sem):
+        pltpu.make_async_copy(ref, ref, sem).wait()
+
+    for load in loads[:4]:
         load.wait()
     go_z(0, 0)
+    go_x(2, 0)
+    go_cross(0, 0)
+    go_x(0, 0)
+    go_z(1, 0)
     go_x(1, 0)
-    go_z(1, 0)
-    go_x(0, 0)
     go_sibling(0, 0)
     go_sibling(1, 0)
-    loads[2].wait()
-
+    for load in loads[4:7]:
+        load.wait()
     for peer in tok_peers:
         pltpu.make_async_remote_copy(
             src_ref=kept.at[tok], dst_ref=kept.at[tok], send_sem=bulk_s.at[0], recv_sem=bulk_r.at[0],
             device_id={"tok": peer}, device_id_type=MESH,
         ).start()
-
-    def settle(ref, sem):
-        pltpu.make_async_copy(ref, ref, sem).wait()
+    factor[0] = (2 * sgn[...] - 1).astype(F32) * scl[...]
+    factor_copy = pltpu.make_async_remote_copy(
+        src_ref=factor.at[0], dst_ref=factor.at[1], send_sem=bulk_s.at[5], recv_sem=bulk_r.at[5],
+        device_id=cross, device_id_type=MESH,
+    )
+    factor_copy.start()
+
+    spots = lax.broadcasted_iota(jnp.int32, (kept_n, tokens), 1)
+    places = spots + jnp.where(spots < 2 * block, col * block, jnp.where(spots < 3 * block, block, (give - 3) * block))
 
     def sign_rows(j, carry):
-        owner = bit_parity(j & tok)
+        owner = jnp.where(spots < 3 * block, bit_parity(j & tok), bit_parity(j & other_tok))
         column = diagonal_column(kept[j].astype(F32), kept_n).astype(jnp.int32)
-        places = lax.broadcasted_iota(jnp.int32, (kept_n, tokens), 1)
         parity = bit_parity(jnp.broadcast_to(column, (kept_n, tokens)) & places) ^ owner
         table[pl.ds(pl.multiple_of(j * kept_n, kept_n), kept_n), :] = (1 - 2 * parity).astype(F32).astype(BF16)
         return carry
@@ -195,50 +232,96 @@
     def ring(r):
         return [(1 + (r + 1) % 2, d) for d in offsets((r + 1) // 2)]
 
-    for k in range(1, 2 * far + 1):
+    waiting = {"main": [(0, 0)], "near": [(1, 0)], "guest": []}
+
+    def work(ready, least):
+        for group in ("main", "near", "guest"):
+            items = ready[group]
+            if len(items) >= least:
+                unit(group, items)
+                waiting[group] = waiting[group][len(items) :]
+
+    def partner_blocks(k):
+        for d in offsets(k - 1):
+            from_x(0, d)
+            go_cross(1, d)
+            go_sibling(3, d)
+
+    def own_blocks(k):
+        for d in offsets(k):
+            from_z(0, d)
+            go_z(0, d)
+            go_x(0, d)
+            go_cross(0, d)
+            if k < far - 1:
+                go_x(1, d)
+            go_sibling(0, d)
+            waiting["main"].append((0, d))
+        if k == far:
+            for d in offsets(far - 1) + offsets(far):
+                go_x(1, d)
+
+    last = 2 * far
+    for k in range(1, last + 1):
+        ready = {group: list(items) for group, items in waiting.items()}
+        if k < far:
+            partner_blocks(k)
         if k <= far:
-            for d in offsets(k):
-                from_z(0, d)
-                go_z(0, d)
-                go_x(0, d)
-                go_sibling(0, d)
-            if k == 1:
-                from_x(2, 0)
-                go_sibling(2, 0)
-                go_z(2, 0)
-            else:
-                for item, d in ring(k - 1):
-                    go_z(item, d)
+            own_blocks(k)
+        if far <= k <= far + 1:
+            partner_blocks(k)
+        if k == 1:
+            from_x(2, 0)
+            go_z(2, 0)
+            go_sibling(2, 0)
+            waiting["near"].append((2, 0))
+        elif k <= far:
+            for item, d in ring(k - 1):
+                go_z(item, d)
         for item, d in ring(k):
             from_z(item, d)
             if k >= far:
                 go_z(item, d)
             go_sibling(item, d)
-        if k <= far + 1:
-            for d in offsets(k - 1):
-                from_x(3, d)
-                go_sibling(3, d)
+            waiting["near"].append((item, d))
+        straight = k - 1 if k < far else {last - 1: far - 1, last: far}.get(k)
+        if straight is not None:
+            for d in offsets(straight):
+                from_x(1, d)
+                go_sibling(4, d)
+                waiting["main"].append((3, d))
+        for kind in (0, 1):
+            if 0 <= k - 1 - kind <= far:
+                for d in offsets(k - 1 - kind):
+                    from_cross(kind, d)
+                    go_sibling(5 + kind, d)
+                    waiting["guest"].append((5 + kind, d))
         if k == 1:
             settle(kept.at[pl.ds(0, tok_n - 1)], bulk_s.at[0])
             settle(kept.at[pl.ds(0, tok_n - 1)], bulk_r.at[0])
+            factor_copy.wait()
             lax.fori_loop(0, tok_n, sign_rows, 0)
-            for load in loads[3:]:
+            for load in loads[7:]:
                 load.wait()
-            unit([(0, 0), (0, 1), (0, -1)], 0, True)
-        elif k <= far + 2:
-            unit(([(0, d) for d in offsets(k)] if k <= far else []) + [(3, d) for d in offsets(k - 2)], 0)
-        if k == 2:
-            unit([(1, 0), (2, 0)] + ring(1), 1, True)
-        elif k % 2 == 0:
-            unit(ring(k - 2) + (ring(k - 1) if k < 2 * far else []), 1)
-    unit(ring(2 * far - 1) + ring(2 * far), 1)
+        work(ready, 3)
+    work({"main": [], "near": [], "guest": waiting["guest"]}, 1)
+    work({"main": [], "near": waiting["near"], "guest": []}, 1)
+    work({"main": waiting["main"], "near": [], "guest": []}, 1)
+
+    row_factor = jnp.concatenate(
+        [
+            factor[0, :, pl.ds(pl.multiple_of(col * block, block), 2 * block)],
+            factor[0, :, 3 * block :],
+            factor[1, :, pl.ds(pl.multiple_of(give * block, block), block)],
+        ],
+        axis=1,
+    )
 
     def activate(m, carry):
         gate = acc[pl.ds(pl.multiple_of(m * 64, 64), 64), :]
         up = acc[pl.ds(pl.multiple_of(units + m * 64, 64), 64), :]
-        factor = (2 * sgn[...] - 1).astype(F32) * scl[...]
         silu = gate / (1.0 + jnp.exp(-gate))
-        hidden[pl.ds(pl.multiple_of(m * 64, 64), 64), :] = (factor * silu * up).astype(BF16)
+        hidden[pl.ds(pl.multiple_of(m * 64, 64), 64), :] = (row_factor * silu * up).astype(BF16)
         return carry
 
     lax.fori_loop(0, units // 64, activate, 0)
@@ -333,13 +416,15 @@
         in_specs=[hbm] * 6,
         out_specs=pl.BlockSpec(memory_space=pltpu.VMEM),
         scratch_shapes=[
-            pltpu.VMEM((hid_n // 2, 2, 2, tokens // 2, width), BF16),
+            pltpu.VMEM((hid_n // 2, 2, 4, tokens // 4, width), BF16),
+            pltpu.VMEM((hid_n // 2, 2, tokens // 4, width), BF16),
             pltpu.VMEM((2 * units, depth), BF16),
             pltpu.VMEM((2 * units, tokens), F32),
             pltpu.VMEM((kept_n * tok_n, tokens), BF16),
             pltpu.VMEM((units, tokens), BF16),
             pltpu.VMEM((1, tokens), jnp.int32),
             pltpu.VMEM((1, tokens), F32),
+            pltpu.VMEM((2, 1, tokens), F32),
             pltpu.VMEM((tok_n, 1, kept_n), jnp.int32),
             pltpu.VMEM((tok_n, kept_n * units // 128, 128), BF16),
             pltpu.VMEM((tok_n, kept_n * units // 128, 128), BF16),
@@ -347,15 +432,17 @@
             pltpu.VMEM((hid_n, 8, tile_lanes), F32),
             pltpu.VMEM((hid_n, 8, tile_lanes), F32),
             pltpu.VMEM((hid_n, 8, tile_lanes), F32),
-            dma((7,)),
+            dma((9,)),
             dma((2, far, 3)),
             dma((2, far, 3)),
-            dma((2 * far + 1,)),
-            dma((2 * far + 1,)),
-            dma((4, 2 * far)),
-            dma((4, 2 * far)),
-            dma((5,)),
-            dma((5,)),
+            dma((3, 2 * far)),
+            dma((3, 2 * far)),
+            dma((2, 2 * far)),
+            dma((2, 2 * far)),
+            dma((7, 2 * far)),
+            dma((7, 2 * far)),
+            dma((6,)),
+            dma((6,)),
         ],
         compiler_params=pltpu.CompilerParams(
             collective_id=0, has_side_effects=True, vmem_limit_bytes=60 * 1024 * 1024

time: 78 us -> 81.6 us (1.046)
  Pallas kernels: 76.4 us -> 79.9 us
    pallas_call x1, Pallas kernels: 76.4 us -> 79.9 us  [per_device(): pl.pallas_call(functools.partial(fused, tok_n, hid_n, float(tokens * tok_...]
where the time goes in v5:
time: 81.6 us; the launch traced here: 81.5 us
  Pallas kernels  79.9 us (98%)
  local copies, waits for them, and re-layouts  1.57 us (2%)
    pallas_call x1, Pallas kernels, per_device(): pl.pallas_call(functools.partial(fused, tok_n, hid_n, float(tokens * tok_...  79.9 us

profile of v5, /device:TPU:1, one launch (start us, length us, event | category | flops | bytes accessed | tf_op | source)
XLA Modules:
  0.0 81.5 jit_solution(8630741013517451931)
XLA Ops:
  0.0 79.9 %sketch_gram.1 = f32[64,512]{1,0:T(8,128)} custom-call(bf16[1024,128]{1,0:T(8,128)(2,1)} %act_in.1, bf16[448,4096]{1,0:T(8,128)(2,1)} %bitcast.5, bf16[448,4096]{1,0:T(8,128)(2,1)} %bitcast.6, s32[1,1024]{1,0:T(1,128)} %bitcast.7, f32[1,1024]{1,0:T(1,128)} %bitcast.8, s32[1,64]{1,0:T(1,128)} %bitcast.9), custom_call_target="tpu_custom_call" | custom-call | tf_op jit(solution)/shard_map/sketch_gram/pallas_call | solution.py:413
  79.9 1.6 %copy.8 = f32[64,512]{1,0:T(8,128)} copy(f32[64,512]{1,0:T(8,128)} %sketch_gram.1) | data formatting | bytes 262144

commit v6 on v5

--- a/solution.py
+++ b/solution.py
@@ -117,8 +117,7 @@
         return d if d >= 0 else far - d
 
     def z_piece(item, d):
-        shard = act.at[chip(item < 2, d), core]
-        return shard.at[pl.ds(0, 3)] if item == 0 else shard.at[3]
+        return act.at[chip(item < 4, d), core, (give, keep, 1, 3, 3)[item]]
 
     def go_z(item, d):
         if 0 <= d < far:
@@ -174,23 +173,24 @@
 
     started = set()
 
-    def unit(group, items):
-        for item, d in items:
-            for part_item in (3, 4) if item == 3 else (item,):
-                from_sibling(part_item, d)
+    def jobs_of(group, items):
         shards = [chip(item in (0, 1, 6), d) for item, d in items]
         first = group not in started
         started.add(group)
-        if group == "main":
-            def tile(m, carry):
-                multiply(shards, lambda q, c: act[q, c, col + m], pl.multiple_of(m * block, block), first)
-                return carry
-
-            lax.fori_loop(0, 2, tile, 0)
-        elif group == "near":
-            multiply(shards, lambda q, c: act[q, c, 3], 2 * block, first)
-        else:
-            multiply(shards, lambda q, c: guest[q, c], 3 * block, first)
+
+        def come():
+            for item, d in items:
+                for part_item in (3, 4) if item == 3 else (item,):
+                    from_sibling(part_item, d)
+
+        if group == "near":
+            return [lambda: (come(), multiply(shards, lambda q, c: act[q, c, 3], 2 * block, first))]
+        if group == "guest":
+            return [lambda: (come(), multiply(shards, lambda q, c: guest[q, c], 3 * block, first))]
+        return [
+            lambda: (come(), multiply(shards, lambda q, c: act[q, c, col], 0, first)),
+            lambda: multiply(shards, lambda q, c: act[q, c, col + 1], block, first),
+        ]
 
     def settle(ref, sem):
         pltpu.make_async_copy(ref, ref, sem).wait()
@@ -200,8 +200,10 @@
     go_z(0, 0)
     go_x(2, 0)
     go_cross(0, 0)
+    go_z(1, 0)
     go_x(0, 0)
-    go_z(1, 0)
+    go_z(2, 0)
+    go_z(3, 0)
     go_x(1, 0)
     go_sibling(0, 0)
     go_sibling(1, 0)
@@ -230,16 +232,20 @@
         return carry
 
     def ring(r):
-        return [(1 + (r + 1) % 2, d) for d in offsets((r + 1) // 2)]
+        return [(3 + (r + 1) % 2, d) for d in offsets((r + 1) // 2)]
 
     waiting = {"main": [(0, 0)], "near": [(1, 0)], "guest": []}
 
-    def work(ready, least):
-        for group in ("main", "near", "guest"):
-            items = ready[group]
-            if len(items) >= least:
-                unit(group, items)
-                waiting[group] = waiting[group][len(items) :]
+    jobs = []
+
+    def plan(group, items):
+        jobs.extend(jobs_of(group, items))
+        waiting[group] = waiting[group][len(items) :]
+
+    def run(count):
+        for job in jobs[:count]:
+            job()
+        del jobs[:count]
 
     def partner_blocks(k):
         for d in offsets(k - 1):
@@ -248,22 +254,28 @@
             go_sibling(3, d)
 
     def own_blocks(k):
-        for d in offsets(k):
-            from_z(0, d)
-            go_z(0, d)
-            go_x(0, d)
-            go_cross(0, d)
-            if k < far - 1:
-                go_x(1, d)
-            go_sibling(0, d)
-            waiting["main"].append((0, d))
+        for item in range(3):
+            for d in offsets(k):
+                from_z(item, d)
+                go_z(item, d)
+                if item == 0:
+                    go_x(0, d)
+                elif item == 1:
+                    go_cross(0, d)
+                else:
+                    if k < far - 1:
+                        go_x(1, d)
+                    go_sibling(0, d)
+                    waiting["main"].append((0, d))
         if k == far:
             for d in offsets(far - 1) + offsets(far):
                 go_x(1, d)
 
     last = 2 * far
     for k in range(1, last + 1):
-        ready = {group: list(items) for group, items in waiting.items()}
+        for group in ("main", "near", "guest"):
+            if len(waiting[group]) >= (3 if k < last else 1):
+                plan(group, list(waiting[group]))
         if k < far:
             partner_blocks(k)
         if k <= far:
@@ -272,18 +284,19 @@
             partner_blocks(k)
         if k == 1:
             from_x(2, 0)
-            go_z(2, 0)
+            go_z(4, 0)
             go_sibling(2, 0)
             waiting["near"].append((2, 0))
         elif k <= far:
             for item, d in ring(k - 1):
                 go_z(item, d)
+        run(len(jobs) if k >= last - 1 else 1)
         for item, d in ring(k):
             from_z(item, d)
             if k >= far:
                 go_z(item, d)
-            go_sibling(item, d)
-            waiting["near"].append((item, d))
+            go_sibling(item - 2, d)
+            waiting["near"].append((item - 2, d))
         straight = k - 1 if k < far else {last - 1: far - 1, last: far}.get(k)
         if straight is not None:
             for d in offsets(straight):
@@ -303,10 +316,11 @@
             lax.fori_loop(0, tok_n, sign_rows, 0)
             for load in loads[7:]:
                 load.wait()
-        work(ready, 3)
-    work({"main": [], "near": [], "guest": waiting["guest"]}, 1)
-    work({"main": [], "near": waiting["near"], "guest": []}, 1)
-    work({"main": waiting["main"], "near": [], "guest": []}, 1)
+        run(len(jobs))
+    for group in ("guest", "near", "main"):
+        if waiting[group]:
+            plan(group, list(waiting[group]))
+    run(len(jobs))
 
     row_factor = jnp.concatenate(
         [
@@ -433,8 +447,8 @@
             pltpu.VMEM((hid_n, 8, tile_lanes), F32),
             pltpu.VMEM((hid_n, 8, tile_lanes), F32),
             dma((9,)),
-            dma((2, far, 3)),
-            dma((2, far, 3)),
+            dma((2, far, 5)),
+            dma((2, far, 5)),
             dma((3, 2 * far)),
             dma((3, 2 * far)),
             dma((2, 2 * far)),

time: 81.6 us -> 79 us (0.968)
  Pallas kernels: 79.9 us -> 77.3 us
    pallas_call x1, Pallas kernels: 79.9 us -> 77.3 us  [per_device(): pl.pallas_call(functools.partial(fused, tok_n, hid_n, float(tokens * tok_...]
where the time goes in v6:
time: 79 us; the launch traced here: 78.9 us
  Pallas kernels  77.3 us (98%)
  local copies, waits for them, and re-layouts  1.57 us (2%)
    pallas_call x1, Pallas kernels, per_device(): pl.pallas_call(functools.partial(fused, tok_n, hid_n, float(tokens * tok_...  77.3 us

profile of v6, /device:TPU:1, one launch (start us, length us, event | category | flops | bytes accessed | tf_op | source)
XLA Modules:
  0.0 78.9 jit_solution(9365270893991712403)
XLA Ops:
  0.0 77.3 %sketch_gram.1 = f32[64,512]{1,0:T(8,128)} custom-call(bf16[1024,128]{1,0:T(8,128)(2,1)} %act_in.1, bf16[448,4096]{1,0:T(8,128)(2,1)} %bitcast.5, bf16[448,4096]{1,0:T(8,128)(2,1)} %bitcast.6, s32[1,1024]{1,0:T(1,128)} %bitcast.7, f32[1,1024]{1,0:T(1,128)} %bitcast.8, s32[1,64]{1,0:T(1,128)} %bitcast.9), custom_call_target="tpu_custom_call" | custom-call | tf_op jit(solution)/shard_map/sketch_gram/pallas_call | solution.py:427
  77.3 1.6 %copy.8 = f32[64,512]{1,0:T(8,128)} copy(f32[64,512]{1,0:T(8,128)} %sketch_gram.1) | data formatting | bytes 262144

commit v7 on v6

--- a/solution.py
+++ b/solution.py
@@ -187,10 +187,12 @@
             return [lambda: (come(), multiply(shards, lambda q, c: act[q, c, 3], 2 * block, first))]
         if group == "guest":
             return [lambda: (come(), multiply(shards, lambda q, c: guest[q, c], 3 * block, first))]
-        return [
-            lambda: (come(), multiply(shards, lambda q, c: act[q, c, col], 0, first)),
-            lambda: multiply(shards, lambda q, c: act[q, c, col + 1], block, first),
-        ]
+
+        def tile(m, carry):
+            multiply(shards, lambda q, c: act[q, c, col + m], pl.multiple_of(m * block, block), first)
+            return carry
+
+        return [lambda: (come(), lax.fori_loop(0, 2, tile, 0))]
 
     def settle(ref, sem):
         pltpu.make_async_copy(ref, ref, sem).wait()
@@ -263,13 +265,9 @@
                 elif item == 1:
                     go_cross(0, d)
                 else:
-                    if k < far - 1:
-                        go_x(1, d)
+                    go_x(1, d)
                     go_sibling(0, d)
                     waiting["main"].append((0, d))
-        if k == far:
-            for d in offsets(far - 1) + offsets(far):
-                go_x(1, d)
 
     last = 2 * far
     for k in range(1, last + 1):
@@ -297,7 +295,7 @@
                 go_z(item, d)
             go_sibling(item - 2, d)
             waiting["near"].append((item - 2, d))
-        straight = k - 1 if k < far else {last - 1: far - 1, last: far}.get(k)
+        straight = k - 1 if k <= far + 1 else None
         if straight is not None:
             for d in offsets(straight):
                 from_x(1, d)

time: 79 us -> 77.5 us (0.981)
  Pallas kernels: 77.3 us -> 75.9 us
    pallas_call x1, Pallas kernels: 77.3 us -> 75.9 us  [per_device(): pl.pallas_call(functools.partial(fused, tok_n, hid_n, float(tokens * tok_...]
where the time goes in v7:
time: 77.5 us; the launch traced here: 77.4 us
  Pallas kernels  75.9 us (98%)
  local copies, waits for them, and re-layouts  1.57 us (2%)
    pallas_call x1, Pallas kernels, per_device(): pl.pallas_call(functools.partial(fused, tok_n, hid_n, float(tokens * tok_...  75.9 us
    unnamed x1, local copies, waits for them, and re-layouts  1.57 us

profile of v7, /device:TPU:1, one launch (start us, length us, event | category | flops | bytes accessed | tf_op | source)
XLA Modules:
  0.0 77.4 jit_solution(1309503560787199875)
XLA Ops:
  0.0 75.9 %sketch_gram.1 = f32[64,512]{1,0:T(8,128)} custom-call(bf16[1024,128]{1,0:T(8,128)(2,1)} %act_in.1, bf16[448,4096]{1,0:T(8,128)(2,1)} %bitcast.5, bf16[448,4096]{1,0:T(8,128)(2,1)} %bitcast.6, s32[1,1024]{1,0:T(1,128)} %bitcast.7, f32[1,1024]{1,0:T(1,128)} %bitcast.8, s32[1,64]{1,0:T(1,128)} %bitcast.9), custom_call_target="tpu_custom_call" | custom-call | tf_op jit(solution)/shard_map/sketch_gram/pallas_call | solution.py:425
  75.9 1.6 %copy.8 = f32[64,512]{1,0:T(8,128)} copy(f32[64,512]{1,0:T(8,128)} %sketch_gram.1) | data formatting | bytes 262144

commit v8 on v7

--- a/solution.py
+++ b/solution.py
@@ -67,10 +67,21 @@
     def ring_order(n):
         return sorted(range(n), key=lambda step: -min(step, n - step))
 
-    hid_peers = [
-        (lax.rem(col + a, 2) * zn + lax.rem(z + step, zn)) * 2 + lax.rem(core + c, 2)
-        for step in ring_order(zn) for a in (1, 0) for c in (1, 0) if step or a or c
-    ]
+    def to_hid_peers(start_copy):
+        def start_four(step, skip_self):
+            for a in (1, 0):
+                for c in (1, 0):
+                    if a or c or not skip_self:
+                        shard = lax.rem(col + a, 2) * zn + lax.rem(z + step, zn)
+                        start_copy(shard * 2 + lax.rem(core + c, 2))
+
+        def ring_step(i, carry):
+            start_four(far + (1 - 2 * lax.rem(i, 2)) * lax.div(i + 1, 2), False)
+            return carry
+
+        lax.fori_loop(0, zn - 1, ring_step, 0)
+        start_four(0, True)
+
     yn = tok_n // 2
     tok_peers = [
         lax.rem(lax.div(tok, 2) + step, yn) * 2 + lax.rem(tok + a, 2)
@@ -330,13 +341,13 @@
     )
 
     def activate(m, carry):
-        gate = acc[pl.ds(pl.multiple_of(m * 64, 64), 64), :]
-        up = acc[pl.ds(pl.multiple_of(units + m * 64, 64), 64), :]
+        gate = acc[pl.ds(pl.multiple_of(m * 16, 16), 16), :]
+        up = acc[pl.ds(pl.multiple_of(units + m * 16, 16), 16), :]
         silu = gate / (1.0 + jnp.exp(-gate))
-        hidden[pl.ds(pl.multiple_of(m * 64, 64), 64), :] = (row_factor * silu * up).astype(BF16)
+        hidden[pl.ds(pl.multiple_of(m * 16, 16), 16), :] = (row_factor * silu * up).astype(BF16)
         return carry
 
-    lax.fori_loop(0, units // 64, activate, 0)
+    lax.fori_loop(0, units // 16, activate, 0)
 
     strips = units // 128
 
@@ -378,8 +389,8 @@
             device_id={"tok": peer}, device_id_type=MESH,
         ).start()
     settle(sk.at[pl.ds(0, tok_n - 1)], bulk_r.at[2])
-    every = jnp.concatenate([unpacked(sk[j].astype(F32)).astype(BF16) for j in range(tok_n)], axis=0)
-    gram = lax.dot_general(unpacked(mine.astype(F32)).astype(BF16), every, (((1,), (1,)), ((), ())), preferred_element_type=F32) * gram_scale
+    every = jnp.concatenate([unpacked(sk[j]) for j in range(tok_n)], axis=0)
+    gram = lax.dot_general(unpacked(mine), every, (((1,), (1,)), ((), ())), preferred_element_type=F32) * gram_scale
 
     tile_rows, tile_lanes = gs.shape[1:]
     across_n = gram.shape[1] // tile_lanes
@@ -387,20 +398,24 @@
         a, b = divmod(t, across_n)
         gs[t] = gram[a * tile_rows : (a + 1) * tile_rows, b * tile_lanes : (b + 1) * tile_lanes]
 
-    for peer in hid_peers:
+    def send_tile(peer):
         pltpu.make_async_remote_copy(
             src_ref=gs.at[peer], dst_ref=gr.at[hid], send_sem=bulk_s.at[3], recv_sem=bulk_r.at[3],
             device_id={"hid": peer}, device_id_type=MESH,
         ).start()
+
+    to_hid_peers(send_tile)
     gr[hid] = gs[hid]
     settle(gr.at[pl.ds(0, hid_n - 1)], bulk_r.at[3])
     gf[hid] = jnp.sum(gr[...], axis=0)
 
-    for peer in hid_peers:
+    def send_sum(peer):
         pltpu.make_async_remote_copy(
             src_ref=gf.at[hid], dst_ref=gf.at[hid], send_sem=bulk_s.at[4], recv_sem=bulk_r.at[4],
             device_id={"hid": peer}, device_id_type=MESH,
         ).start()
+
+    to_hid_peers(send_sum)
     for copy in sends:
         copy.wait_send()
     settle(part.at[pl.ds(0, tok_n - 1)], bulk_s.at[1])

time: 77.5 us -> 78 us (level)
  no operation moved by 1% of the time
where the time goes in v8:
time: 78 us; the launch traced here: 77.9 us
  Pallas kernels  76.3 us (98%)
  local copies, waits for them, and re-layouts  1.57 us (2%)
    pallas_call x1, Pallas kernels, per_device(): pl.pallas_call(functools.partial(fused, tok_n, hid_n, float(tokens * tok_...  76.3 us
    unnamed x1, local copies, waits for them, and re-layouts  1.57 us

profile of v8, /device:TPU:1, one launch (start us, length us, event | category | flops | bytes accessed | tf_op | source)
XLA Modules:
  0.0 77.9 jit_solution(5823104064422718766)
XLA Ops:
  0.0 76.3 %sketch_gram.1 = f32[64,512]{1,0:T(8,128)} custom-call(bf16[1024,128]{1,0:T(8,128)(2,1)} %act_in.1, bf16[448,4096]{1,0:T(8,128)(2,1)} %bitcast.5, bf16[448,4096]{1,0:T(8,128)(2,1)} %bitcast.6, s32[1,1024]{1,0:T(1,128)} %bitcast.7, f32[1,1024]{1,0:T(1,128)} %bitcast.8, s32[1,64]{1,0:T(1,128)} %bitcast.9), custom_call_target="tpu_custom_call" | custom-call | tf_op jit(solution)/shard_map/sketch_gram/pallas_call | solution.py:440
  76.4 1.6 %copy.8 = f32[64,512]{1,0:T(8,128)} copy(f32[64,512]{1,0:T(8,128)} %sketch_gram.1) | data formatting | bytes 262144
